TPU v7x, 256 devices: a whole 4x4x8 slice. The times are simulated.
256 devices in a mesh: row: 32 (over y, z_lo, core), col: 8 (over x, z_hi).
Axes of the slice: x: 4, y: 4, z: 8 (z_hi: 2, z_lo: 4; z = z_hi * 4 + z_lo), core: 2. Of those that a mesh axis runs over, the one named last changes fastest.
Arguments:
- weight: float32 [8192, 4096], P('row', 'col'), may hold values from -0.0625 to 0.0625
- grad: bfloat16 [8192, 4096], P('row', 'col'), may hold values from -6 to 6
- left: bfloat16 [8192, 8192], P('row', 'col'), may hold values from -0.25 to 3, as said below
- right: bfloat16 [4096, 4096], P('row', 'col'), may hold values from -0.25 to 3, as said below
- tokens: bfloat16 [4096, 8192], P('row'), may hold values from -6 to 6
Outputs:
- new_weight: float32 [8192, 4096], P('row', 'col')
- output: bfloat16 [4096, 4096], P('row', 'col')
Inputs may be any that keep to these rules, and one draw needn't show every extreme that they name: left is symmetric. right is symmetric.
All inputs are finite; a program needn't handle non-finite values.
Results may differ from a plain program's by a relative error of at most 0.0056.
Values may be sent and summed in bfloat16 or wider, within the bound.
A program may use at most 64 MiB of HBM per device.

v0:
```python
import jax
import jax.numpy as jnp
from jax import lax
from jax.sharding import PartitionSpec as P


def shards(weight, grad, left, right, tokens):
    left_panel = lax.all_gather(left, "col", axis=1, tiled=True)
    left_total = jnp.dot(
        left_panel,
        lax.all_gather(grad, "row", axis=0, tiled=True),
        preferred_element_type=jnp.float32,
    )
    left_grad = left_total.astype(jnp.bfloat16)
    right_panel = lax.all_gather(right, "row", axis=0, tiled=True)
    selected = right_panel
    precond = lax.psum_scatter(
        lax.dot_general(
            selected, left_grad, (((1,), (1,)), ((), ())), preferred_element_type=jnp.float32
        ),
        "col",
        scatter_dimension=0,
        tiled=True,
    ).T
    new_weight = weight - 0.01 * precond
    narrow = new_weight.astype(jnp.bfloat16)
    spread = lax.all_to_all(tokens, "row", split_axis=1, concat_axis=0, tiled=True)
    selected = spread
    output = lax.psum_scatter(
        jnp.dot(selected, narrow, preferred_element_type=jnp.float32),
        "row",
        scatter_dimension=0,
        tiled=True,
    )
    return (new_weight, output.astype(jnp.bfloat16))


def solution(mesh):
    return jax.shard_map(
        shards,
        mesh=mesh,
        in_specs=(
            P("row", "col"),
            P("row", "col"),
            P("row", "col"),
            P("row", "col"),
            P("row", None),
        ),
        out_specs=(P("row", "col"), P("row", "col")),
        check_vma=False,
    )
```

profile of v0, /device:TPU:4, one launch (start us, length us, event | category | flops | bytes accessed | tf_op | source)
XLA Modules:
  0.0 573.1 jit_solution(13484413524477637766)
XLA Ops:
  7.2 0.0 all-gather.4.cloned.1.call-start
  7.2 0.7 all-gather.4.cloned.1.call-update
  7.9 0.0 all-gather.8.cloned.1.call-start
  7.9 0.7 all-gather.8.cloned.1.call-update
  8.6 0.0 all-gather.6.cloned.1.call-start
  8.7 0.7 all-gather.6.cloned.1.call-update
  9.4 0.0 reduce-scatter.3.cloned.1.call-start
  9.4 109.7 %all-gather.4.cloned.1.call-done = bf16[256,8192]{1,0:T(8,128)(2,1)} async-done(((bf16[256,1024]{1,0:T(8,128)(2,1)}), bf16[256,8192]{1,0:T(8,128)(2,1)}) %all-gather.4.cloned.1.call-update) | async-done | bytes 4194320 | tf_op jit(solution)/shard_map/all_gather | solution.py:8
  119.1 60.5 %all-gather.8.cloned.1.call-done = bf16[4096,512]{1,0:T(8,128)(2,1)} async-done(((bf16[128,512]{1,0:T(8,128)(2,1)}), bf16[4096,512]{1,0:T(8,128)(2,1)}) %all-gather.8.cloned.1.call-update) | async-done | bytes 4194320 | tf_op jit(solution)/shard_map/all_gather | solution.py:15
  179.6 69.8 %all-gather.6.cloned.1.call-done = bf16[8192,512]{1,0:T(8,128)(2,1)} async-done(((bf16[256,512]{1,0:T(8,128)(2,1)}), bf16[8192,512]{1,0:T(8,128)(2,1)}) %all-gather.6.cloned.1.call-update) | async-done | bytes 8388624 | tf_op jit(solution)/shard_map/all_gather | solution.py:11
  249.4 11.2 %convolution_bitcast_fusion.1 = f32[4096,256]{0,1:T(8,128)} fusion(bf16[4096,512]{1,0:T(8,128)(2,1)} %all-gather.8.cloned.1.call-done, bf16[256,8192]{1,0:T(8,128)(2,1)} %all-gather.4.cloned.1.call-done, bf16[8192,512]{1,0:T(8,128)(2,1)} %all-gather.6.cloned.1.call-done), kind=kOutput, calls=%fused_computation.1 | convolution fusion | flops 3221356544 | bytes 20971520 | tf_op jit(solution)/shard_map/dot_general | solution.py:18
  260.6 0.0 copy-start
  260.6 0.0 reduce-scatter.3.cloned.1.call-update
  260.6 0.0 reduce-scatter.5.cloned.1.call-start
  260.7 1.5 copy-done
  262.2 2.4 copy.9
  264.6 0.0 copy-start.2
  264.6 100.4 %all_to_all.19 = bf16[128,32,256]{0,2,1:T(8,128)(2,1)S(1)} all-to-all(bf16[128,32,256]{0,2,1:T(8,128)(2,1)} %bitcast.14), channel_id=1, replica_groups=mesh['row'=32,'col'=8] {'row'}, dimensions={1} | all-to-all | bytes 4194304 | tf_op jit(solution)/shard_map/all_to_all | solution.py:27
  365.1 2.9 copy.10
  368.0 27.8 %reduce-scatter.3.cloned.1.call-done = f32[512,256]{0,1:T(8,128)} async-done(((f32[4096,256]{0,1:T(8,128)}), f32[512,256]{0,1:T(8,128)}) %reduce-scatter.3.cloned.1.call-update) | async-done | bytes 524304 | tf_op jit(solution)/shard_map/reduce_scatter | solution.py:17
  395.7 0.0 copy-done.2
  395.7 1.1 bitcast_subtract_fusion
  396.9 0.0 copy-start.1
  396.9 6.3 %convolution_bitcast_fusion = f32[4096,512]{0,1:T(8,128)} fusion(bf16[4096,256]{1,0:T(8,128)(2,1)} %bitcast.15, f32[256,512]{1,0:T(8,128)S(1)} %bitcast_subtract_fusion), kind=kOutput, calls=%fused_computation | convolution fusion | flops 1073872896 | bytes 11010048 | tf_op jit(solution)/shard_map/dot_general | solution.py:30
  403.2 0.0 copy-done.1
  403.2 0.0 reduce-scatter.5.cloned.1.call-update
  403.2 161.6 %reduce-scatter.5.cloned.1.call-done = f32[128,512]{0,1:T(8,128)} async-done(((f32[4096,512]{0,1:T(8,128)}), f32[128,512]{0,1:T(8,128)}) %reduce-scatter.5.cloned.1.call-update) | async-done | bytes 262160 | tf_op jit(solution)/shard_map/reduce_scatter | solution.py:29
  564.9 1.0 convert_element_type.11
  565.8 0.8 copy.11
Async XLA Ops:
  7.2 112.0 %all-gather.4.cloned.1.call-start = ((), (), s32[]{:S(2)}) async-start(), calls=%async_computation.3 | async-start | bytes 4718592 | tf_op jit(solution)/shard_map/all_gather | solution.py:8
  7.9 171.7 %all-gather.8.cloned.1.call-start = ((), (), s32[]{:S(2)}) async-start(), calls=%async_computation.5 | async-start | bytes 4325376 | tf_op jit(solution)/shard_map/all_gather | solution.py:15
  8.6 240.7 %all-gather.6.cloned.1.call-start = ((), (), s32[]{:S(2)}) async-start(), calls=%async_computation.4 | async-start | bytes 8650752 | tf_op jit(solution)/shard_map/all_gather | solution.py:11
  9.4 386.4 %reduce-scatter.3.cloned.1.call-start = ((), (), s32[]{:S(2)}) async-start(), calls=%async_computation.6 | async-start | bytes 4718592 | tf_op jit(solution)/shard_map/reduce_scatter | solution.py:17
  260.6 1.6 copy-start
  260.6 304.2 %reduce-scatter.5.cloned.1.call-start = ((), (), s32[]{:S(2)}) async-start(), calls=%async_computation.7 | async-start | bytes 8650752 | tf_op jit(solution)/shard_map/reduce_scatter | solution.py:29
  264.6 131.1 %copy-start.2 = (f32[256,512]{1,0:T(8,128)S(1)}, f32[256,512]{1,0:T(8,128)}, u32[]{:S(2)}) copy-start(f32[256,512]{1,0:T(8,128)} %param.5) | copy-start | bytes 1572868
  396.9 6.3 %copy-start.1 = (f32[256,512]{1,0:T(8,128)}, f32[256,512]{1,0:T(8,128)S(1)}, u32[]{:S(2)}) copy-start(f32[256,512]{1,0:T(8,128)S(1)} %bitcast_subtract_fusion) | copy-start | bytes 1572868
Sparse Core Ops, SparseCore 0:
  10.6 108.4 all-gather.3
  121.0 58.5 all-gather.7
  181.5 67.8 all-gather.5
  260.7 134.9 reduce-scatter.2
  403.3 161.4 reduce-scatter.4
where the time goes:
time: 573 us
  waiting for transfers between devices  431 us (75%)
  blocking collectives  100 us (17%)
  matrix products  17.5 us (3%)
  between operations  13.8 us (2%)
  local copies, waits for them, and re-layouts  7.66 us (1%)
    reduce_scatter x1, waiting for transfers between devices, shards(): lax.psum_scatter(jnp.dot(selected, narrow, preferred_element_type=jnp.flo...  162 us
    all_gather x1, waiting for transfers between devices, shards(): left_panel = lax.all_gather(left, 'col', axis=1, tiled=True)  110 us
    all_to_all x1, blocking collectives, shards(): lax.all_to_all(tokens, 'row', split_axis=1, concat_axis=0, tiled=True)  100 us
    all_gather x1, waiting for transfers between devices, shards(): lax.all_gather(grad, 'row', axis=0, tiled=True)  69.8 us
    all_gather x1, waiting for transfers between devices, shards(): right_panel = lax.all_gather(right, 'row', axis=0, tiled=True)  60.5 us
    reduce_scatter x1, waiting for transfers between devices, shards(): lax.psum_scatter(lax.dot_general(selected, left_grad, (((1,), (1,)), ((),...  27.8 us
  transfers between devices with their start and end apart: 5, of which 5 were waited for; matrix products, arithmetic and copies ran while one was open for 1% of the time, Pallas kernels for 0%

commit v1 on v0

--- a/solution.py
+++ b/solution.py
@@ -2,6 +2,15 @@
 import jax.numpy as jnp
 from jax import lax
 from jax.sharding import PartitionSpec as P
+
+
+def axis_part_launch(local, axis_tag, dimension_no, d_out):
+    return jnp.concatenate(
+        lax.all_to_all(
+            jnp.stack(jnp.split(local, lax.psum(1, axis_tag), dimension_no)), axis_tag, 0, 0
+        ),
+        d_out,
+    )
 
 
 def shards(weight, grad, left, right, tokens):
@@ -24,7 +33,7 @@
     ).T
     new_weight = weight - 0.01 * precond
     narrow = new_weight.astype(jnp.bfloat16)
-    spread = lax.all_to_all(tokens, "row", split_axis=1, concat_axis=0, tiled=True)
+    spread = axis_part_launch(tokens, "row", 1, 0)
     selected = spread
     output = lax.psum_scatter(
         jnp.dot(selected, narrow, preferred_element_type=jnp.float32),

time: 573 us -> 569 us (level)
  blocking collectives: 100 us -> 0 us
  waiting for transfers between devices: 431 us -> 502 us
  local copies, waits for them, and re-layouts: 7.66 us -> 28.7 us
    all_to_all x1 -> x0, blocking collectives: 100 us -> none  [shards(): lax.all_to_all(tokens, 'row', split_axis=1, concat_axis=0, tiled=True)]
    reduce_scatter x1, waiting for transfers between devices: 27.8 us -> 114 us  [shards(): lax.psum_scatter(lax.dot_general(selected, left_grad, (((1,), (1,)), ((),...]
    unnamed x8 -> x37, local copies, waits for them, and re-layouts: 4.73 us -> 28.1 us
    all_gather x1, waiting for transfers between devices: 110 us -> 94.3 us  [shards(): left_panel = lax.all_gather(left, 'col', axis=1, tiled=True)]
  transfers between devices with their start and end apart: 5 -> 6, of which waited for: 5 -> 5; matrix products, arithmetic and copies ran while one was open for 1% -> 5% of each run, Pallas kernels for 0% -> 0%
where the time goes in v1:
time: 569 us
  waiting for transfers between devices  502 us (88%)
  local copies, waits for them, and re-layouts  28.7 us (5%)
  matrix products  15.7 us (3%)
  between operations  13.8 us (2%)
    reduce_scatter x1, waiting for transfers between devices, shards(): lax.psum_scatter(jnp.dot(selected, narrow, preferred_element_type=jnp.flo...  162 us
    reduce_scatter x1, waiting for transfers between devices, shards(): lax.psum_scatter(lax.dot_general(selected, left_grad, (((1,), (1,)), ((),...  114 us
    all_gather x1, waiting for transfers between devices, shards(): left_panel = lax.all_gather(left, 'col', axis=1, tiled=True)  94.3 us
    all_gather x1, waiting for transfers between devices, shards(): lax.all_gather(grad, 'row', axis=0, tiled=True)  69.8 us
    all_gather x1, waiting for transfers between devices, shards(): right_panel = lax.all_gather(right, 'row', axis=0, tiled=True)  60.5 us
    unnamed x37, local copies, waits for them, and re-layouts  28.1 us
  transfers between devices with their start and end apart: 6, of which 5 were waited for; matrix products, arithmetic and copies ran while one was open for 5% of the time, Pallas kernels for 0%

profile of v1, /device:TPU:4, one launch (start us, length us, event | category | flops | bytes accessed | tf_op | source)
XLA Modules:
  0.0 568.5 jit_solution(5597614680891131559)
XLA Ops:
  7.2 0.7 all-gather.4.cloned.1.call-update
  7.9 0.0 all-gather.8.cloned.1.call-start
  8.0 0.7 all-gather.8.cloned.1.call-update
  8.7 0.7 all-gather.6.cloned.1.call-update
  9.4 0.0 reduce-scatter.3.cloned.1.call-start
  9.4 1.5 constant_dynamic-update-slice_fusion.31
  10.9 1.5 constant_dynamic-update-slice_fusion.30
  12.4 1.5 constant_dynamic-update-slice_fusion.29
  13.9 1.5 constant_dynamic-update-slice_fusion.28
  15.3 1.5 constant_dynamic-update-slice_fusion.27
  16.8 1.5 constant_dynamic-update-slice_fusion.26
  18.3 1.5 constant_dynamic-update-slice_fusion.25
  19.7 1.5 constant_dynamic-update-slice_fusion.24
  21.2 1.5 constant_dynamic-update-slice_fusion.23
  22.7 1.5 constant_dynamic-update-slice_fusion.22
  24.2 0.6 constant_dynamic-update-slice_fusion.21
  24.8 94.3 %all-gather.4.cloned.1.call-done = bf16[256,8192]{1,0:T(8,128)(2,1)} async-done(((bf16[256,1024]{1,0:T(8,128)(2,1)}), bf16[256,8192]{1,0:T(8,128)(2,1)}) %all-gather.4.cloned.1.call-update) | async-done | bytes 4194320 | tf_op jit(solution)/shard_map/all_gather | solution.py:17
  119.1 60.5 %all-gather.8.cloned.1.call-done = bf16[4096,512]{1,0:T(8,128)(2,1)} async-done(((bf16[128,512]{1,0:T(8,128)(2,1)}), bf16[4096,512]{1,0:T(8,128)(2,1)}) %all-gather.8.cloned.1.call-update) | async-done | bytes 4194320 | tf_op jit(solution)/shard_map/all_gather | solution.py:24
  179.6 69.8 %all-gather.6.cloned.1.call-done = bf16[8192,512]{1,0:T(8,128)(2,1)} async-done(((bf16[256,512]{1,0:T(8,128)(2,1)}), bf16[8192,512]{1,0:T(8,128)(2,1)}) %all-gather.6.cloned.1.call-update) | async-done | bytes 8388624 | tf_op jit(solution)/shard_map/all_gather | solution.py:20
  249.4 11.2 %convolution_bitcast_fusion = f32[4096,256]{0,1:T(8,128)} fusion(bf16[4096,512]{1,0:T(8,128)(2,1)} %all-gather.8.cloned.1.call-done, bf16[256,8192]{1,0:T(8,128)(2,1)} %all-gather.4.cloned.1.call-done, bf16[8192,512]{1,0:T(8,128)(2,1)} %all-gather.6.cloned.1.call-done), kind=kOutput, calls=%fused_computation | convolution fusion | flops 3221356544 | bytes 20971520 | tf_op jit(solution)/shard_map/dot_general | solution.py:27
  260.6 0.6 constant_dynamic-update-slice_fusion.20
  261.3 0.6 constant_dynamic-update-slice_fusion.19
  261.9 0.6 constant_dynamic-update-slice_fusion.18
  262.5 0.6 constant_dynamic-update-slice_fusion.17
  263.2 0.6 constant_dynamic-update-slice_fusion.16
  263.8 0.6 constant_dynamic-update-slice_fusion.15
  264.4 0.7 constant_dynamic-update-slice_fusion.14
  265.1 0.6 constant_dynamic-update-slice_fusion.13
  265.7 0.6 constant_dynamic-update-slice_fusion.12
  266.4 0.6 constant_dynamic-update-slice_fusion.11
  267.0 0.6 constant_dynamic-update-slice_fusion.10
  267.7 0.6 constant_dynamic-update-slice_fusion.9
  268.3 0.6 constant_dynamic-update-slice_fusion.8
  268.9 0.6 constant_dynamic-update-slice_fusion.7
  269.6 0.6 constant_dynamic-update-slice_fusion.6
  270.2 0.6 constant_dynamic-update-slice_fusion.5
  270.9 0.6 constant_dynamic-update-slice_fusion.4
  271.5 0.6 constant_dynamic-update-slice_fusion.3
  272.1 0.6 constant_dynamic-update-slice_fusion.2
  272.8 0.6 constant_dynamic-update-slice_fusion.1
  273.4 0.6 constant_dynamic-update-slice_fusion
  274.0 5.2 all-to-all-start
  279.2 0.0 reduce-scatter.5.cloned.1.call-start
  279.3 113.8 %reduce-scatter.3.cloned.1.call-done = f32[512,256]{0,1:T(8,128)} async-done(((f32[4096,256]{0,1:T(8,128)}), f32[512,256]{0,1:T(8,128)}) %reduce-scatter.3.cloned.1.call-update) | async-done | bytes 524304 | tf_op jit(solution)/shard_map/reduce_scatter | solution.py:26
  393.1 1.1 bitcast_subtract_fusion
  394.2 4.5 fusion
  398.7 161.6 %reduce-scatter.5.cloned.1.call-done = f32[128,512]{1,0:T(8,128)} async-done(((f32[4096,512]{1,0:T(8,128)}), f32[128,512]{1,0:T(8,128)}) %reduce-scatter.5.cloned.1.call-update) | async-done | bytes 262160 | tf_op jit(solution)/shard_map/reduce_scatter | solution.py:38
  560.4 1.6 convert_element_type.11
  (11 shorter events, 0.1 us)
Async XLA Ops:
  7.2 17.0 %copy-start.1 = (bf16[128,8192]{1,0:T(8,128)(2,1)S(1)}, bf16[128,8192]{1,0:T(8,128)(2,1)}, u32[]{:S(2)}) copy-start(bf16[128,8192]{1,0:T(8,128)(2,1)} %param.9) | copy-start | bytes 6291460
  7.2 112.0 %all-gather.4.cloned.1.call-start = ((), (), s32[]{:S(2)}) async-start(), calls=%async_computation.3 | async-start | bytes 4718592 | tf_op jit(solution)/shard_map/all_gather | solution.py:17
  7.9 171.7 %all-gather.8.cloned.1.call-start = ((), (), s32[]{:S(2)}) async-start(), calls=%async_computation.5 | async-start | bytes 4325376 | tf_op jit(solution)/shard_map/all_gather | solution.py:24
  8.7 240.7 %all-gather.6.cloned.1.call-start = ((), (), s32[]{:S(2)}) async-start(), calls=%async_computation.4 | async-start | bytes 8650752 | tf_op jit(solution)/shard_map/all_gather | solution.py:20
  9.4 383.7 %reduce-scatter.3.cloned.1.call-start = ((), (), s32[]{:S(2)}) async-start(), calls=%async_computation.6 | async-start | bytes 4718592 | tf_op jit(solution)/shard_map/reduce_scatter | solution.py:26
  274.0 119.0 %copy-start.2 = (f32[256,512]{1,0:T(8,128)S(1)}, f32[256,512]{1,0:T(8,128)}, u32[]{:S(2)}) copy-start(f32[256,512]{1,0:T(8,128)} %param.5) | copy-start | bytes 1572868
  274.0 120.2 %all-to-all-start = ((bf16[32,128,256]{2,1,0:T(8,128)(2,1)}), bf16[32,128,256]{2,1,0:T(8,128)(2,1)S(1)}, u32[]{:S(2)}, u32[]{:S(2)}) async-start(bf16[32,128,256]{2,1,0:T(8,128)(2,1)} %constant_dynamic-update-slice_fusion), calls=%async_computation.1 | async-start | bytes 4194304 | tf_op jit(solution)/shard_map/all_to_all | solution.py:9
  279.2 281.2 %reduce-scatter.5.cloned.1.call-start = ((), (), s32[]{:S(2)}) async-start(), calls=%async_computation.7 | async-start | bytes 8650752 | tf_op jit(solution)/shard_map/reduce_scatter | solution.py:38
  394.2 4.5 copy-start
Sparse Core Ops, SparseCore 0:
  10.6 108.4 all-gather.3
  121.0 58.5 all-gather.7
  181.5 67.8 all-gather.5
  260.8 132.2 reduce-scatter.2
  398.9 161.4 reduce-scatter.4
